TPU v7x, 32 devices: a whole 2x2x4 slice. The times are simulated.
32 devices in a mesh: groups: 2 (over y), wide: 8 (over z, x), narrow: 2 (over core).
Axes of the slice: x: 2, y: 2, z: 4, core: 2. Of those that a mesh axis runs over, the one named last changes fastest.
Arguments:
- goals: float32 [8192, 1024], P(('groups', 'wide', 'narrow')), parts along dimension 0, may hold values from -32 to 32
- premises: float32 [1024, 1024], P(('groups', 'wide', 'narrow')), parts along dimension 0, may hold values from -24 to 24
- counts: int32 [8192], P(('groups', 'wide')), parts along dimension 0, may hold values from 1 to 16
- positives: int32 [8192, 16], P(('groups', 'wide')), parts along dimension 0, may hold values from -1 to 511, as said below
- cotangent: float32 [8192], P(('groups', 'wide')), parts along dimension 0, may hold values from -6 to 6
Outputs:
- goal_loss: float32 [8192], P(('groups', 'wide')), parts along dimension 0
- grad_goals: float32 [8192, 1024], P(('groups', 'wide', 'narrow')), parts along dimension 0
- grad_premises: float32 [1024, 1024], P(('groups', 'wide', 'narrow')), parts along dimension 0
There are 2 independent parts, one for each index of `groups`. A program takes and returns all parts, laid end to end along the dimension named above; each array names one. Nothing has to cross between parts.
Inputs may be any that keep to these rules, and one draw needn't show every extreme that they name: positives[i, k] is a premise index for k < counts[i] and -1 from there on.
All inputs are finite; a program needn't handle non-finite values.
Results may differ from a plain program's by a relative error of at most 0.012.
The roundings to bfloat16 on the way count: a program that leaves them out, or rounds other values in their place, can miss the bound.
Values may be sent and summed in bfloat16 or wider, within the bound.
A program may use at most 64 MiB of HBM per device.

v0:
```python
import jax
import jax.numpy as jnp
from jax import lax
from jax.sharding import PartitionSpec as P


def hit_counts(row_lists, column_ids):
    total = jnp.zeros((row_lists.shape[0], column_ids.shape[0]), jnp.float32)
    for which_slot in range(row_lists.shape[1]):
        total = total + (row_lists[:, which_slot][:, None] == column_ids[None, :]).astype(
            jnp.float32
        )
    return total


def per_device(goals, premises, counts, positives, cotangent):
    goal_part = goals.astype(jnp.bfloat16)
    prem_part = premises.astype(jnp.bfloat16)
    prem_rows = prem_part.shape[0]
    width = goal_part.shape[1]
    scale = width ** (-0.5)
    n_wide = lax.axis_size("wide")
    n_narrow = lax.axis_size("narrow")
    narrow_index = lax.axis_index("narrow")
    rows_block = lax.all_gather(goal_part, "narrow", axis=0, tiled=True)
    prem_block = lax.all_gather(prem_part, "wide", axis=0, tiled=True)
    goal_counts = counts.astype(jnp.float32)
    local_ids = jnp.arange(prem_rows * n_wide, dtype=jnp.int32)
    column_ids = (
        local_ids // prem_rows * n_narrow + narrow_index
    ) * prem_rows + local_ids % prem_rows
    col_total = prem_block.shape[0]
    row_total = rows_block.shape[0]
    step_cols = 512 if col_total % 512 == 0 else col_total
    starts = list(range(0, col_total, step_cols))

    def tile_scores(begin):
        piece = prem_block[begin : begin + step_cols]
        return (
            lax.dot_general(
                rows_block, piece, (((1,), (1,)), ((), ())), preferred_element_type=jnp.float32
            )
            * scale
        )

    top = jnp.full((row_total,), -jnp.inf, jnp.float32)
    total = jnp.zeros((row_total,), jnp.float32)
    positive_sum = jnp.zeros((row_total,), jnp.float32)
    for begin in starts:
        scores = tile_scores(begin)
        hits = hit_counts(positives, column_ids[begin : begin + step_cols])
        new_top = jnp.maximum(top, jnp.max(scores, axis=1))
        total = total * jnp.exp(top - new_top) + jnp.sum(jnp.exp(scores - new_top[:, None]), axis=1)
        positive_sum = positive_sum + jnp.sum(hits * scores, axis=1)
        top = new_top
    best = lax.pmax(top, "narrow")
    total_all, positive_all = lax.psum((total * jnp.exp(top - best), positive_sum), "narrow")
    log_total = best + jnp.log(total_all)
    row_loss = log_total - positive_all / goal_counts
    grad_rows = jnp.zeros((row_total, width), jnp.float32)
    pieces = []
    for number, begin in enumerate(starts):
        scores = tile_scores(begin)
        hits = hit_counts(positives, column_ids[begin : begin + step_cols])
        dscores = (
            cotangent[:, None]
            * (jnp.exp(scores - log_total[:, None]) - hits / goal_counts[:, None])
            * scale
        ).astype(jnp.bfloat16)
        grad_rows = grad_rows + jnp.dot(
            dscores, prem_block[begin : begin + step_cols], preferred_element_type=jnp.float32
        )
        pieces.append(dscores)
    stored = jnp.concatenate(pieces, axis=1)
    grad_goals = lax.psum_scatter(grad_rows, "narrow", scatter_dimension=0, tiled=True)
    grad_premises = lax.psum_scatter(
        lax.dot_general(
            stored, rows_block, (((0,), (0,)), ((), ())), preferred_element_type=jnp.float32
        ),
        "wide",
        scatter_dimension=0,
        tiled=True,
    )
    return (row_loss, grad_goals, grad_premises)


def solution(mesh):
    return jax.shard_map(
        per_device,
        mesh=mesh,
        in_specs=(
            P(("groups", "wide", "narrow"), None),
            P(("groups", "wide", "narrow"), None),
            P(("groups", "wide")),
            P(("groups", "wide"), None),
            P(("groups", "wide")),
        ),
        out_specs=(
            P(("groups", "wide")),
            P(("groups", "wide", "narrow"), None),
            P(("groups", "wide", "narrow"), None),
        ),
        check_vma=False,
    )
```

profile of v0, /device:TPU:0, one launch (start us, length us, event | category | flops | bytes accessed | tf_op | source)
XLA Modules:
  0.0 136.1 jit_solution(13301415830657365863)
XLA Ops:
  7.2 0.0 copy-start.2
  7.2 0.0 copy-start
  7.2 0.0 copy-start.1
  7.2 0.0 all-gather.2.cloned.1.call-start
  7.2 2.1 %convert_element_type.76 = bf16[256,1024]{1,0:T(8,128)(2,1)} convert(f32[256,1024]{1,0:T(8,128)} %param.5) | non-fusion elementwise | flops 262144 | bytes 1572864 | tf_op jit(solution)/shard_map/convert_element_type | solution.py:17
  9.4 0.0 copy-start.4
  9.4 0.0 all-gather.2.cloned.1.call-update
  9.4 0.0 reduce-scatter.5.cloned.1.call-start
  9.4 0.0 copy-done.2
  9.5 0.0 copy-done
  9.5 0.0 copy-done.1
  9.6 33.0 %all_gather.7 = bf16[256,1024]{1,0:T(8,128)(2,1)S(1)} all-gather(bf16[32,1024]{1,0:T(8,128)(2,1)S(1)} %convert_element_type.77), channel_id=1, replica_groups=mesh['groups'=2,'wide'=8,'narrow'=2] {'wide'}, dimensions={0}, use_global_device_ids=true | all-gather | bytes 589824 | tf_op jit(solution)/shard_map/all_gather | solution.py:26
  42.6 0.0 all-gather.2.cloned.1.call-done
  42.6 0.0 copy-start.3
  42.6 1.8 %fusion.9 = (f32[512]{0:T(512)S(1)}, f32[512,256]{0,1:T(8,128)S(1)}) fusion(bf16[512,1024]{1,0:T(8,128)(2,1)} %all-gather.2.cloned.1.call-done, bf16[256,1024]{1,0:T(8,128)(2,1)S(1)} %all_gather.7), kind=kOutput, calls=%fused_computation.22 | convolution fusion | flops 268697088 | bytes 2099200 | tf_op jit(solution)/shard_map/dot_general | solution.py:40
  44.4 2.5 %pmax.7 = f32[512]{0:T(512)S(1)} all-reduce(f32[512]{0:T(512)S(1)} %get-tuple-element.25), channel_id=1, replica_groups=mesh['groups'=2,'wide'=8,'narrow'=2] {'narrow'}, use_global_device_ids=true, to_apply=%region_1.2 | all-reduce | flops 512 | bytes 4096 | tf_op jit(solution)/shard_map/pmax | solution.py:56
  46.9 1.1 multiply_reduce_fusion
  47.9 2.5 %all-reduce = (f32[512]{0:T(512)S(1)}, f32[512]{0:T(512)S(1)}) all-reduce(f32[512]{0:T(512)S(1)} %exponential_multiply_fusion, f32[512]{0:T(512)S(1)} %get-tuple-element.3), channel_id=1, replica_groups=mesh['groups'=2,'wide'=8,'narrow'=2] {'narrow'}, use_global_device_ids=true, to_apply=%region_3.4 | all-reduce | flops 1024 | bytes 8192 | tf_op jit(solution)/shard_map/psum | solution.py:57
  50.4 0.6 divide_subtract_fusion
  51.0 0.0 copy-done.4
  51.0 0.0 copy-done.3
  51.0 2.3 %fusion.6 = f32[256,1024]{1,0:T(8,128)} fusion(bf16[512,1024]{1,0:T(8,128)(2,1)S(1)} %copy-done.3, f32[512,256]{0,1:T(8,128)S(1)} %get-tuple-element.26, f32[512]{0:T(512)S(1)} %convert_element_type.94, f32[512]{0:T(512)S(1)} %get-tuple-element.8, f32[512]{0:T(512)S(1)} %copy-done.4, s32[512]{0:T(512)S(1)} %bitcast.63, s32[512]{0:T(512)S(1)} %bitcast.66, ...), kind=kOutput, calls=%fused_computation.19 | convolution fusion | flops 275382272 | bytes 2661376 | tf_op jit(solution)/shard_map/dot_general | solution.py:77
  53.3 0.0 reduce-scatter.5.cloned.1.call-update
  53.3 0.0 reduce-scatter.3.cloned.1.call-start
  53.4 2.7 %fusion.7 = f32[512,1024]{1,0:T(8,128)} fusion(bf16[256,1024]{1,0:T(8,128)(2,1)S(1)} %all_gather.7, f32[512,256]{0,1:T(8,128)S(1)} %get-tuple-element.26, f32[512]{0:T(512)S(1)} %convert_element_type.94, f32[512]{0:T(512)S(1)} %get-tuple-element.8, f32[512]{0:T(512)S(1)} %copy-done.4, s32[512]{0:T(512)S(1)} %bitcast.64, s32[512]{0:T(512)S(1)} %bitcast.67, ...), kind=kOutput, calls=%fused_computation.20 | convolution fusion | flops 275382272 | bytes 3185664 | tf_op jit(solution)/shard_map/dot_general | solution.py:70
  56.1 0.0 reduce-scatter.3.cloned.1.call-update
  56.1 61.9 %reduce-scatter.5.cloned.1.call-done = f32[32,1024]{1,0:T(8,128)} async-done(((f32[256,1024]{1,0:T(8,128)}), f32[32,1024]{1,0:T(8,128)}) %reduce-scatter.5.cloned.1.call-update) | async-done | bytes 131088 | tf_op jit(solution)/shard_map/reduce_scatter | solution.py:76
  118.0 11.6 %reduce-scatter.3.cloned.1.call-done = f32[256,1024]{1,0:T(8,128)} async-done(((f32[512,1024]{1,0:T(8,128)}), f32[256,1024]{1,0:T(8,128)}) %reduce-scatter.3.cloned.1.call-update) | async-done | bytes 1048592 | tf_op jit(solution)/shard_map/reduce_scatter | solution.py:75
  (5 shorter events, 0.1 us)
Async XLA Ops:
  7.2 2.3 %copy-start.2 = (s32[512]{0:T(512)S(1)}, s32[512]{0:T(512)}, u32[]{:S(2)}) copy-start(s32[512]{0:T(512)} %param.7) | copy-start | bytes 6148
  7.2 2.3 %copy-start = (f32[32,1024]{1,0:T(8,128)S(1)}, f32[32,1024]{1,0:T(8,128)}, u32[]{:S(2)}) copy-start(f32[32,1024]{1,0:T(8,128)} %param.6) | copy-start | bytes 393220
  7.2 2.3 %copy-start.1 = (s32[512,16]{0,1:T(8,128)S(1)}, s32[512,16]{0,1:T(8,128)}, u32[]{:S(2)}) copy-start(s32[512,16]{0,1:T(8,128)} %param.8) | copy-start | bytes 98308
  7.2 35.4 %all-gather.2.cloned.1.call-start = ((), (), s32[]{:S(2)}) async-start(), calls=%async_computation.2 | async-start | bytes 1572864 | tf_op jit(solution)/shard_map/all_gather | solution.py:25
  9.4 41.6 %copy-start.4 = (f32[512]{0:T(512)S(1)}, f32[512]{0:T(512)}, u32[]{:S(2)}) copy-start(f32[512]{0:T(512)} %param.9) | copy-start | bytes 6148
  9.4 108.6 %reduce-scatter.5.cloned.1.call-start = ((), (), s32[]{:S(2)}) async-start(), calls=%async_computation.4 | async-start | bytes 1179648 | tf_op jit(solution)/shard_map/reduce_scatter | solution.py:76
  42.6 8.4 %copy-start.3 = (bf16[512,1024]{1,0:T(8,128)(2,1)S(1)}, bf16[512,1024]{1,0:T(8,128)(2,1)}, u32[]{:S(2)}) copy-start(bf16[512,1024]{1,0:T(8,128)(2,1)} %all-gather.2.cloned.1.call-done) | copy-start | bytes 3145732
  53.3 76.3 %reduce-scatter.3.cloned.1.call-start = ((), (), s32[]{:S(2)}) async-start(), calls=%async_computation.3 | async-start | bytes 3145728 | tf_op jit(solution)/shard_map/reduce_scatter | solution.py:75
Sparse Core Ops, SparseCore 0:
  10.1 11.7 all-gather.1
  53.4 64.5 reduce-scatter.4
  120.9 8.6 reduce-scatter.2
where the time goes:
time: 136 us
  waiting for transfers between devices  73.5 us (54%)
  blocking collectives  38 us (28%)
  between operations  13.8 us (10%)
  matrix products  6.82 us (5%)
  other arithmetic  3.82 us (3%)
    reduce_scatter x1, waiting for transfers between devices, per_device(): lax.psum_scatter(lax.dot_general(stored, rows_block, (((0,), (0,)), ((),...  61.9 us
    all_gather x1, blocking collectives, per_device(): prem_block = lax.all_gather(prem_part, 'wide', axis=0, tiled=True)  33 us
    reduce_scatter x1, waiting for transfers between devices, per_device(): lax.psum_scatter(grad_rows, 'narrow', scatter_dimension=0, tiled=True)  11.6 us
    dot_general x1, matrix products, per_device(): jnp.dot(dscores, prem_block[begin:begin + step_cols], preferred_element_t...  2.73 us
  transfers between devices with their start and end apart: 3, of which 2 were waited for; matrix products, arithmetic and copies ran while one was open for 2% of the time, Pallas kernels for 0%

commit v1 on v0

--- a/solution.py
+++ b/solution.py
@@ -2,6 +2,23 @@
 import jax.numpy as jnp
 from jax import lax
 from jax.sharding import PartitionSpec as P
+
+
+def laid_out(tiles, dim):
+    tiles = jnp.moveaxis(tiles, 0, dim)
+    dims = tiles.shape
+    return tiles.reshape(*dims[:dim], dims[dim] * dims[dim + 1], *dims[dim + 2 :])
+
+
+def ring_gather(x, axis, dim):
+    devices = lax.axis_size(axis)
+    ahead = [(i, (i + 1) % devices) for i in range(devices)]
+    blocks = [x]
+    while len(blocks) < devices:
+        blocks.append(lax.ppermute(blocks[-1], axis, ahead))
+    place = lax.axis_index(axis)
+    blocks = jnp.stack(blocks)[(place - jnp.arange(devices)) % devices]
+    return laid_out(blocks, dim)
 
 
 def hit_counts(row_lists, column_ids):
@@ -23,7 +40,7 @@
     n_narrow = lax.axis_size("narrow")
     narrow_index = lax.axis_index("narrow")
     rows_block = lax.all_gather(goal_part, "narrow", axis=0, tiled=True)
-    prem_block = lax.all_gather(prem_part, "wide", axis=0, tiled=True)
+    prem_block = ring_gather(prem_part, "wide", 0)
     goal_counts = counts.astype(jnp.float32)
     local_ids = jnp.arange(prem_rows * n_wide, dtype=jnp.int32)
     column_ids = (

time: 136 us -> 151 us (1.11)
  waiting for transfers between devices: 73.5 us -> 117 us
  blocking collectives: 38 us -> 4.94 us
  starting transfers between devices: 0.12 us -> 3.13 us
    ppermute x0 -> x7, waiting for transfers between devices: none -> 47.3 us  [ring_gather(): blocks.append(lax.ppermute(blocks[-1], axis, ahead))]
    all_gather x1 -> x0, blocking collectives: 33 us -> none  [per_device(): prem_block = lax.all_gather(prem_part, 'wide', axis=0, tiled=True)]
    reduce_scatter x1, waiting for transfers between devices: 61.9 us -> 58.3 us  [per_device(): lax.psum_scatter(lax.dot_general(stored, rows_block, (((0,), (0,)), ((),...]
    ppermute x0 -> x7, starting transfers between devices: none -> 3.01 us  [ring_gather(): blocks.append(lax.ppermute(blocks[-1], axis, ahead))]
  transfers between devices with their start and end apart: 3 -> 10, of which waited for: 2 -> 9; matrix products, arithmetic and copies ran while one was open for 2% -> 2% of each run, Pallas kernels for 0% -> 0%
where the time goes in v1:
time: 151 us
  waiting for transfers between devices  117 us (77%)
  between operations  13.9 us (9%)
  matrix products  6.82 us (5%)
  blocking collectives  4.94 us (3%)
  other arithmetic  3.83 us (3%)
  starting transfers between devices  3.13 us (2%)
    reduce_scatter x1, waiting for transfers between devices, per_device(): lax.psum_scatter(lax.dot_general(stored, rows_block, (((0,), (0,)), ((),...  58.3 us
    ppermute x7, waiting for transfers between devices, ring_gather(): blocks.append(lax.ppermute(blocks[-1], axis, ahead))  47.3 us
    reduce_scatter x1, waiting for transfers between devices, per_device(): lax.psum_scatter(grad_rows, 'narrow', scatter_dimension=0, tiled=True)  11.6 us
  transfers between devices with their start and end apart: 10, of which 9 were waited for; matrix products, arithmetic and copies ran while one was open for 2% of the time, Pallas kernels for 0%

profile of v1, /device:TPU:0, one launch (start us, length us, event | category | flops | bytes accessed | tf_op | source)
XLA Modules:
  0.0 150.5 jit_solution(14446924091594846674)
XLA Ops:
  7.2 0.0 copy-start.1
  7.2 0.0 copy-start.3
  7.2 0.0 copy-start.2
  7.2 0.0 all-gather.2.cloned.1.call-start
  7.2 2.1 %convert_element_type.77 = bf16[256,1024]{1,0:T(8,128)(2,1)} convert(f32[256,1024]{1,0:T(8,128)} %param.5) | non-fusion elementwise | flops 262144 | bytes 1572864 | tf_op jit(solution)/shard_map/convert_element_type | solution.py:34
  9.4 0.0 all-gather.2.cloned.1.call-update
  9.4 0.0 reduce-scatter.5.cloned.1.call-start
  9.4 0.0 copy-done.1
  9.5 3.0 %collective-permute-start = (bf16[32,1024]{1,0:T(8,128)(2,1)S(1)}, bf16[32,1024]{1,0:T(8,128)(2,1)S(1)}, u32[]{:S(2)}, u32[]{:S(2)}) collective-permute-start(bf16[32,1024]{1,0:T(8,128)(2,1)S(1)} %get-tuple-element.10), channel_id=1, source_target_pairs={{0,2},{2,4},{4,6},{6,8},{8,10},{10,12},{12,14},{14,0},{1,3},{3,5},... | collective-permute-start | bytes 196616 | tf_op jit(solution)/shard_map/ppermute | solution.py:18
  12.5 0.0 copy-done.3
  12.5 0.0 copy-done.2
  12.6 5.2 %collective-permute-done = bf16[32,1024]{1,0:T(8,128)(2,1)S(1)} collective-permute-done((bf16[32,1024]{1,0:T(8,128)(2,1)S(1)}, bf16[32,1024]{1,0:T(8,128)(2,1)S(1)}, u32[]{:S(2)}, u32[]{:S(2)}) %collective-permute-start) | collective-permute-done | bytes 65568 | tf_op jit(solution)/shard_map/ppermute | solution.py:18
  17.7 0.0 collective-permute-start.1
  17.7 7.0 %collective-permute-done.1 = bf16[32,1024]{1,0:T(8,128)(2,1)S(1)} collective-permute-done((bf16[32,1024]{1,0:T(8,128)(2,1)S(1)}, bf16[32,1024]{1,0:T(8,128)(2,1)S(1)}, u32[]{:S(2)}, u32[]{:S(2)}) %collective-permute-start.1) | collective-permute-done | bytes 65568 | tf_op jit(solution)/shard_map/ppermute | solution.py:18
  24.7 0.0 collective-permute-start.2
  24.7 7.0 %collective-permute-done.2 = bf16[32,1024]{1,0:T(8,128)(2,1)S(1)} collective-permute-done((bf16[32,1024]{1,0:T(8,128)(2,1)S(1)}, bf16[32,1024]{1,0:T(8,128)(2,1)S(1)}, u32[]{:S(2)}, u32[]{:S(2)}) %collective-permute-start.2) | collective-permute-done | bytes 65568 | tf_op jit(solution)/shard_map/ppermute | solution.py:18
  31.7 0.0 collective-permute-start.3
  31.7 7.0 %collective-permute-done.3 = bf16[32,1024]{1,0:T(8,128)(2,1)S(1)} collective-permute-done((bf16[32,1024]{1,0:T(8,128)(2,1)S(1)}, bf16[32,1024]{1,0:T(8,128)(2,1)S(1)}, u32[]{:S(2)}, u32[]{:S(2)}) %collective-permute-start.3) | collective-permute-done | bytes 65568 | tf_op jit(solution)/shard_map/ppermute | solution.py:18
  38.6 0.0 collective-permute-start.4
  38.6 0.0 copy-start.4
  38.6 7.4 %collective-permute-done.4 = bf16[32,1024]{1,0:T(8,128)(2,1)S(1)} collective-permute-done((bf16[32,1024]{1,0:T(8,128)(2,1)S(1)}, bf16[32,1024]{1,0:T(8,128)(2,1)S(1)}, u32[]{:S(2)}, u32[]{:S(2)}) %collective-permute-start.4) | collective-permute-done | bytes 65568 | tf_op jit(solution)/shard_map/ppermute | solution.py:18
  46.0 0.0 collective-permute-start.5
  46.0 7.0 %collective-permute-done.5 = bf16[32,1024]{1,0:T(8,128)(2,1)S(1)} collective-permute-done((bf16[32,1024]{1,0:T(8,128)(2,1)S(1)}, bf16[32,1024]{1,0:T(8,128)(2,1)S(1)}, u32[]{:S(2)}, u32[]{:S(2)}) %collective-permute-start.5) | collective-permute-done | bytes 65568 | tf_op jit(solution)/shard_map/ppermute | solution.py:18
  53.0 0.0 collective-permute-start.6
  53.0 7.0 %collective-permute-done.6 = bf16[32,1024]{1,0:T(8,128)(2,1)S(1)} collective-permute-done((bf16[32,1024]{1,0:T(8,128)(2,1)S(1)}, bf16[32,1024]{1,0:T(8,128)(2,1)S(1)}, u32[]{:S(2)}, u32[]{:S(2)}) %collective-permute-start.6) | collective-permute-done | bytes 65568 | tf_op jit(solution)/shard_map/ppermute | solution.py:18
  59.9 0.6 gather_fusion
  60.5 0.0 all-gather.2.cloned.1.call-done
  60.6 0.0 copy-start
  60.6 1.8 %fusion.21 = (f32[512]{0:T(512)S(1)}, f32[256,512]{1,0:T(8,128)S(1)}) fusion(bf16[256,1024]{1,0:T(8,128)(2,1)S(1)} %bitcast.61, bf16[512,1024]{1,0:T(8,128)(2,1)} %all-gather.2.cloned.1.call-done), kind=kOutput, calls=%fused_computation.46 | convolution fusion | flops 268697088 | bytes 2099200 | tf_op jit(solution)/shard_map/dot_general | solution.py:57
  62.4 2.5 %pmax.7 = f32[512]{0:T(512)S(1)} all-reduce(f32[512]{0:T(512)S(1)} %get-tuple-element.27), channel_id=1, replica_groups=mesh['groups'=2,'wide'=8,'narrow'=2] {'narrow'}, use_global_device_ids=true, to_apply=%region_1.2 | all-reduce | flops 512 | bytes 4096 | tf_op jit(solution)/shard_map/pmax | solution.py:73
  64.9 1.1 fusion.2
  65.9 2.5 %all-reduce = (f32[512]{0:T(512)S(1)}, f32[512]{0:T(512)S(1)}) all-reduce(f32[512]{0:T(512)S(1)} %exponential_multiply_fusion, f32[512]{0:T(512)S(1)} %get-tuple-element.3), channel_id=1, replica_groups=mesh['groups'=2,'wide'=8,'narrow'=2] {'narrow'}, use_global_device_ids=true, to_apply=%region_3.4 | all-reduce | flops 1024 | bytes 8192 | tf_op jit(solution)/shard_map/psum | solution.py:74
  68.4 0.6 divide_subtract_fusion
  69.0 0.0 copy-done.4
  69.0 0.0 copy-done
  69.0 2.3 %fusion.16 = f32[256,1024]{1,0:T(8,128)} fusion(bf16[512,1024]{1,0:T(8,128)(2,1)S(1)} %copy-done, f32[256,512]{1,0:T(8,128)S(1)} %get-tuple-element.28, f32[512]{0:T(512)S(1)} %convert_element_type.94, f32[512]{0:T(512)S(1)} %get-tuple-element.8, f32[512]{0:T(512)S(1)} %copy-done.4, s32[512]{0:T(512)S(1)} %bitcast.106, s32[512]{0:T(512)S(1)} %bitcast.109, ...), kind=kOutput, calls=%fused_computation.43 | convolution fusion | flops 275382272 | bytes 2661376 | tf_op jit(solution)/shard_map/dot_general | solution.py:94
  71.3 0.0 reduce-scatter.5.cloned.1.call-update
  71.3 0.0 reduce-scatter.3.cloned.1.call-start
  71.4 2.7 %fusion.18 = f32[512,1024]{1,0:T(8,128)} fusion(bf16[256,1024]{1,0:T(8,128)(2,1)S(1)} %bitcast.62, f32[256,512]{1,0:T(8,128)S(1)} %get-tuple-element.28, f32[512]{0:T(512)S(1)} %convert_element_type.94, f32[512]{0:T(512)S(1)} %get-tuple-element.8, f32[512]{0:T(512)S(1)} %copy-done.4, s32[512]{0:T(512)S(1)} %bitcast.107, s32[512]{0:T(512)S(1)} %bitcast.110, ...), kind=kOutput, calls=%fused_computation.44 | convolution fusion | flops 275382272 | bytes 3185664 | tf_op jit(solution)/shard_map/dot_general | solution.py:87
  74.1 0.0 reduce-scatter.3.cloned.1.call-update
  74.1 58.3 %reduce-scatter.5.cloned.1.call-done = f32[32,1024]{1,0:T(8,128)} async-done(((f32[256,1024]{1,0:T(8,128)}), f32[32,1024]{1,0:T(8,128)}) %reduce-scatter.5.cloned.1.call-update) | async-done | bytes 131088 | tf_op jit(solution)/shard_map/reduce_scatter | solution.py:93
  132.4 11.6 %reduce-scatter.3.cloned.1.call-done = f32[256,1024]{1,0:T(8,128)} async-done(((f32[512,1024]{1,0:T(8,128)}), f32[256,1024]{1,0:T(8,128)}) %reduce-scatter.3.cloned.1.call-update) | async-done | bytes 1048592 | tf_op jit(solution)/shard_map/reduce_scatter | solution.py:92
  (14 shorter events, 0.1 us)
Async XLA Ops:
  7.2 2.3 %copy-start.1 = (f32[32,1024]{1,0:T(8,128)S(1)}, f32[32,1024]{1,0:T(8,128)}, u32[]{:S(2)}) copy-start(f32[32,1024]{1,0:T(8,128)} %param.6) | copy-start | bytes 393220
  7.2 5.3 %copy-start.3 = (s32[512]{0:T(512)S(1)}, s32[512]{0:T(512)}, u32[]{:S(2)}) copy-start(s32[512]{0:T(512)} %param.7) | copy-start | bytes 6148
  7.2 5.3 %copy-start.2 = (s32[512,16]{0,1:T(8,128)S(1)}, s32[512,16]{0,1:T(8,128)}, u32[]{:S(2)}) copy-start(s32[512,16]{0,1:T(8,128)} %param.8) | copy-start | bytes 98308
  7.2 53.4 %all-gather.2.cloned.1.call-start = ((), (), s32[]{:S(2)}) async-start(), calls=%async_computation.2 | async-start | bytes 1572864 | tf_op jit(solution)/shard_map/all_gather | solution.py:42
  9.4 123.1 %reduce-scatter.5.cloned.1.call-start = ((), (), s32[]{:S(2)}) async-start(), calls=%async_computation.4 | async-start | bytes 1179648 | tf_op jit(solution)/shard_map/reduce_scatter | solution.py:93
  9.5 8.3 %collective-permute-start = (bf16[32,1024]{1,0:T(8,128)(2,1)S(1)}, bf16[32,1024]{1,0:T(8,128)(2,1)S(1)}, u32[]{:S(2)}, u32[]{:S(2)}) collective-permute-start(bf16[32,1024]{1,0:T(8,128)(2,1)S(1)} %get-tuple-element.10), channel_id=1, source_target_pairs={{0,2},{2,4},{4,6},{6,8},{8,10},{10,12},{12,14},{14,0},{1,3},{3,5},... | collective-permute-start | bytes 196616 | tf_op jit(solution)/shard_map/ppermute | solution.py:18
  17.7 7.0 %collective-permute-start.1 = (bf16[32,1024]{1,0:T(8,128)(2,1)S(1)}, bf16[32,1024]{1,0:T(8,128)(2,1)S(1)}, u32[]{:S(2)}, u32[]{:S(2)}) collective-permute-start(bf16[32,1024]{1,0:T(8,128)(2,1)S(1)} %collective-permute-done), channel_id=1, source_target_pairs={{0,2},{2,4},{4,6},{6,8},{8,10},{10,12},{12,14},{14,0},{1,3},{3,5},... | collective-permute-start | bytes 196616 | tf_op jit(solution)/shard_map/ppermute | solution.py:18
  24.7 7.0 %collective-permute-start.2 = (bf16[32,1024]{1,0:T(8,128)(2,1)S(1)}, bf16[32,1024]{1,0:T(8,128)(2,1)S(1)}, u32[]{:S(2)}, u32[]{:S(2)}) collective-permute-start(bf16[32,1024]{1,0:T(8,128)(2,1)S(1)} %collective-permute-done.1), channel_id=1, source_target_pairs={{0,2},{2,4},{4,6},{6,8},{8,10},{10,12},{12,14},{14,0},{1,3},{3,5},... | collective-permute-start | bytes 196616 | tf_op jit(solution)/shard_map/ppermute | solution.py:18
  31.7 7.0 %collective-permute-start.3 = (bf16[32,1024]{1,0:T(8,128)(2,1)S(1)}, bf16[32,1024]{1,0:T(8,128)(2,1)S(1)}, u32[]{:S(2)}, u32[]{:S(2)}) collective-permute-start(bf16[32,1024]{1,0:T(8,128)(2,1)S(1)} %collective-permute-done.2), channel_id=1, source_target_pairs={{0,2},{2,4},{4,6},{6,8},{8,10},{10,12},{12,14},{14,0},{1,3},{3,5},... | collective-permute-start | bytes 196616 | tf_op jit(solution)/shard_map/ppermute | solution.py:18
  38.6 7.4 %collective-permute-start.4 = (bf16[32,1024]{1,0:T(8,128)(2,1)S(1)}, bf16[32,1024]{1,0:T(8,128)(2,1)S(1)}, u32[]{:S(2)}, u32[]{:S(2)}) collective-permute-start(bf16[32,1024]{1,0:T(8,128)(2,1)S(1)} %collective-permute-done.3), channel_id=1, source_target_pairs={{0,2},{2,4},{4,6},{6,8},{8,10},{10,12},{12,14},{14,0},{1,3},{3,5},... | collective-permute-start | bytes 196616 | tf_op jit(solution)/shard_map/ppermute | solution.py:18
  38.6 30.4 %copy-start.4 = (f32[512]{0:T(512)S(1)}, f32[512]{0:T(512)}, u32[]{:S(2)}) copy-start(f32[512]{0:T(512)} %param.9) | copy-start | bytes 6148
  46.0 7.0 %collective-permute-start.5 = (bf16[32,1024]{1,0:T(8,128)(2,1)S(1)}, bf16[32,1024]{1,0:T(8,128)(2,1)S(1)}, u32[]{:S(2)}, u32[]{:S(2)}) collective-permute-start(bf16[32,1024]{1,0:T(8,128)(2,1)S(1)} %collective-permute-done.4), channel_id=1, source_target_pairs={{0,2},{2,4},{4,6},{6,8},{8,10},{10,12},{12,14},{14,0},{1,3},{3,5},... | collective-permute-start | bytes 196616 | tf_op jit(solution)/shard_map/ppermute | solution.py:18
  53.0 7.0 %collective-permute-start.6 = (bf16[32,1024]{1,0:T(8,128)(2,1)S(1)}, bf16[32,1024]{1,0:T(8,128)(2,1)S(1)}, u32[]{:S(2)}, u32[]{:S(2)}) collective-permute-start(bf16[32,1024]{1,0:T(8,128)(2,1)S(1)} %collective-permute-done.5), channel_id=1, source_target_pairs={{0,2},{2,4},{4,6},{6,8},{8,10},{10,12},{12,14},{14,0},{1,3},{3,5},... | collective-permute-start | bytes 196616 | tf_op jit(solution)/shard_map/ppermute | solution.py:18
  60.6 8.4 %copy-start = (bf16[512,1024]{1,0:T(8,128)(2,1)S(1)}, bf16[512,1024]{1,0:T(8,128)(2,1)}, u32[]{:S(2)}) copy-start(bf16[512,1024]{1,0:T(8,128)(2,1)} %all-gather.2.cloned.1.call-done) | copy-start | bytes 3145732
  71.3 72.7 %reduce-scatter.3.cloned.1.call-start = ((), (), s32[]{:S(2)}) async-start(), calls=%async_computation.3 | async-start | bytes 3145728 | tf_op jit(solution)/shard_map/reduce_scatter | solution.py:92
Sparse Core Ops, SparseCore 0:
  10.1 11.7 all-gather.1
  71.4 60.9 reduce-scatter.4
  135.3 8.6 reduce-scatter.2
